TPU v7x, 128 devices: a whole 4x4x4 slice. The times are simulated.
128 devices in a mesh: row: 8 (over z, core), col: 16 (over y, x).
Axes of the slice: x: 4, y: 4, z: 4, core: 2. Of those that a mesh axis runs over, the one named last changes fastest.
Arguments:
- left_amps: bfloat16 [8192, 8192], P('row', 'col'), may hold values from -6 to 6
- right_ints: bfloat16 [8192, 16384], P('row', 'col'), may hold values from -0.0625 to 0.0625
- left_mask: int32 [64, 64], P('row', 'col'), may hold values from 0 to 1, as said below
- right_mask: int32 [64, 128], P('row', 'col'), may hold values from 0 to 1, as said below
- result_mask: int32 [64, 128], P('row', 'col'), may hold values from 0 to 1, as said below
Outputs:
- pair_major: bfloat16 [128, 1048576], P(None, ('row', 'col'))
Inputs may be any that keep to these rules, and one draw needn't show every extreme that they name: `left_mask`: a tile is kept (1) or left out (0). `right_mask`: a tile is kept (1) or left out (0). `result_mask`: a tile is kept (1) or left out (0).
All inputs are finite; a program needn't handle non-finite values.
Results may differ from a plain program's by a relative error of at most 0.001.
Values may be sent and summed in bfloat16 or wider, within the bound.
A program may use at most 128 MiB of HBM per device.

v0:
```python
import jax
import jax.numpy as jnp
from jax import lax
from jax.sharding import PartitionSpec as P

TILE = 128


def expand(values, mask):
    rows, cols = values.shape
    tiled = values.reshape(rows // TILE, TILE, cols // TILE, TILE)
    kept = tiled * mask.astype(values.dtype)[:, None, :, None]
    return kept.reshape(rows, cols)


def local(left_amps, right_ints, left_mask, right_mask, result_mask):
    masked_left = expand(left_amps, left_mask)
    masked_right = expand(right_ints, right_mask)
    rows_here = masked_left.shape[0]
    cols_here = masked_right.shape[1]
    whole_left = lax.all_gather(masked_left, "col", axis=1, tiled=True)
    product = jnp.dot(
        whole_left,
        lax.all_gather(masked_right, "row", axis=0, tiled=True),
        preferred_element_type=jnp.float32,
    )
    kept = expand(product, result_mask).astype(jnp.bfloat16)
    n_row = lax.axis_size("row")
    n_col = lax.axis_size("col")
    owners = n_row * n_col
    share = rows_here * cols_here // owners
    pieces = kept.reshape(owners, share)
    return lax.all_to_all(pieces, ("row", "col"), split_axis=0, concat_axis=0, tiled=True)


def solution(mesh):
    in_specs = (P("row", "col"), P("row", "col"), P("row", "col"), P("row", "col"), P("row", "col"))
    out_specs = P(None, ("row", "col"))
    return jax.shard_map(local, mesh=mesh, in_specs=in_specs, out_specs=out_specs, check_vma=False)
```

profile of v0, /device:TPU:1, one launch (start us, length us, event | category | flops | bytes accessed | tf_op | source)
XLA Modules:
  0.0 325.5 jit_solution(3875941070786762936)
XLA Ops:
  6.5 0.0 all-gather.5.cloned.1.call-start
  6.5 0.7 convert_element_type.13
  7.2 0.3 mul.36
  7.6 0.0 copy-start.2
  7.6 0.0 copy-start
  7.6 3.3 %bitcast_multiply_fusion.1 = bf16[1024,1024]{1,0:T(8,128)(2,1)} fusion(bf16[1024,1024]{1,0:T(8,128)(2,1)} %param.6, bf16[128,8,8,128]{3,2,1,0:T(8,128)(2,1)S(1)} %bitcast.19), kind=kLoop, calls=%fused_computation.2 | loop fusion | flops 1048576 | bytes 6291456 | tf_op jit(solution)/shard_map/mul | solution.py:12
  10.9 0.0 copy-start.1
  10.9 0.0 all-gather.5.cloned.1.call-update
  10.9 0.0 all-gather.3.cloned.1.call-start
  10.9 0.0 copy-done.2
  11.0 0.1 copy.9
  11.1 0.3 mul.33
  11.4 0.0 copy-done
  11.4 1.2 bitcast_multiply_fusion.2
  12.6 0.0 all-gather.3.cloned.1.call-update
  12.6 0.0 copy-done.1
  12.6 87.2 %all-gather.5.cloned.1.call-done = bf16[8192,1024]{1,0:T(8,128)(2,1)} async-done(((bf16[1024,1024]{1,0:T(8,128)(2,1)}), bf16[8192,1024]{1,0:T(8,128)(2,1)}) %all-gather.5.cloned.1.call-update) | async-done | bytes 16777232 | tf_op jit(solution)/shard_map/all_gather | solution.py:24
  99.9 122.2 %all-gather.3.cloned.1.call-done = bf16[1024,8192]{1,0:T(8,128)(2,1)} async-done(((bf16[1024,512]{1,0:T(8,128)(2,1)}), bf16[1024,8192]{1,0:T(8,128)(2,1)}) %all-gather.3.cloned.1.call-update) | async-done | bytes 16777232 | tf_op jit(solution)/shard_map/all_gather | solution.py:21
  222.1 0.3 mul.39
  222.4 22.4 %fusion = bf16[1024,1024]{1,0:T(8,128)(2,1)S(1)} fusion(f32[128,8,8,128]{3,2,1,0:T(8,128)S(1)} %bitcast.21, bf16[1024,8192]{1,0:T(8,128)(2,1)} %all-gather.3.cloned.1.call-done, bf16[8192,1024]{1,0:T(8,128)(2,1)} %all-gather.5.cloned.1.call-done), kind=kOutput, calls=%fused_computation.1 | convolution fusion | flops 17181966336 | bytes 39845888 | tf_op jit(solution)/shard_map/dot_general | solution.py:22
  244.8 6.5 %all_to_all.11 = bf16[128,1,8192]{2,1,0:T(2,128)(2,1)} reshape(bf16[1024,1024]{1,0:T(8,128)(2,1)S(1)} %fusion) | data formatting | bytes 4194304 | tf_op jit(solution)/shard_map/all_to_all | solution.py:33
  251.3 0.5 broadcast.6
  251.8 13.2 %reduce = bf16[128,8192]{1,0:T(8,128)(2,1)S(1)} reduce(bf16[128,1,8192]{2,1,0:T(2,128)(2,1)} %all_to_all.11, bf16[]{:T(256)} %broadcast.6), dimensions={1}, to_apply=%all_to_all.11.reduce_sub_computation | reduce | bytes 4194306 | tf_op jit(solution)/shard_map/all_to_all | solution.py:33
  265.1 2.8 reshape.16
  267.8 38.3 %all_to_all.13 = bf16[128,2,4096]{2,1,0:T(2,128)(2,1)S(1)} all-to-all(bf16[128,2,4096]{2,1,0:T(2,128)(2,1)} %reshape.16), channel_id=1, replica_groups=mesh['row'=8,'col'=16] {'row','col'}, dimensions={0} | all-to-all | bytes 4194304 | tf_op jit(solution)/shard_map/all_to_all | solution.py:33
  306.1 6.7 %reshape.17 = bf16[128,1,8192]{2,1,0:T(2,128)(2,1)} reshape(bf16[128,2,4096]{2,1,0:T(2,128)(2,1)S(1)} %all_to_all.13) | data formatting | bytes 4194304
  312.8 5.8 %copy.19 = bf16[128,1,8192]{2,0,1:T(8,128)(2,1)} copy(bf16[128,1,8192]{2,1,0:T(2,128)(2,1)} %reshape.17) | data formatting | bytes 4194304
  (2 shorter events, 0.0 us)
Async XLA Ops:
  6.5 93.3 %all-gather.5.cloned.1.call-start = ((), (), s32[]{:S(2)}) async-start(), calls=%async_computation.2 | async-start | bytes 18874368 | tf_op jit(solution)/shard_map/all_gather | solution.py:24
  7.6 3.4 %copy-start.2 = (s32[8,4]{0,1:T(4,128)S(1)}, s32[8,4]{0,1:T(4,128)}, u32[]{:S(2)}) copy-start(s32[8,4]{0,1:T(4,128)} %param.7) | copy-start | bytes 388
  7.6 3.8 %copy-start = (bf16[1024,512]{1,0:T(8,128)(2,1)S(1)}, bf16[1024,512]{1,0:T(8,128)(2,1)}, u32[]{:S(2)}) copy-start(bf16[1024,512]{1,0:T(8,128)(2,1)} %param.5) | copy-start | bytes 3145732
  10.9 1.7 copy-start.1
  10.9 211.2 %all-gather.3.cloned.1.call-start = ((), (), s32[]{:S(2)}) async-start(), calls=%async_computation.1 | async-start | bytes 17825792 | tf_op jit(solution)/shard_map/all_gather | solution.py:21
Sparse Core Ops, SparseCore 0:
  11.0 88.8 all-gather.4
  102.0 120.0 all-gather.2
where the time goes:
time: 326 us; the launch traced here: 325 us
  waiting for transfers between devices  209 us (64%)
  blocking collectives  38.3 us (12%)
  local copies, waits for them, and re-layouts  23.4 us (7%)
  matrix products  22.4 us (7%)
  other arithmetic  18.4 us (6%)
  between operations  13.5 us (4%)
    all_gather x1, waiting for transfers between devices, local(): whole_left = lax.all_gather(masked_left, 'col', axis=1, tiled=True)  122 us
    all_gather x1, waiting for transfers between devices, local(): lax.all_gather(masked_right, 'row', axis=0, tiled=True)  87.2 us
    all_to_all x1, blocking collectives, local(): lax.all_to_all(pieces, ('row', 'col'), split_axis=0, concat_axis=0, tiled...  38.3 us
    dot_general x1, matrix products, local(): jnp.dot(whole_left, lax.all_gather(masked_right, 'row', axis=0, tiled=Tru...  22.4 us
    unnamed x9, local copies, waits for them, and re-layouts  15.3 us
    all_to_all x1, other arithmetic, local(): lax.all_to_all(pieces, ('row', 'col'), split_axis=0, concat_axis=0, tiled...  13.2 us
    all_to_all x2, local copies, waits for them, and re-layouts, local(): lax.all_to_all(pieces, ('row', 'col'), split_axis=0, concat_axis=0, tiled...  7.03 us
  transfers between devices with their start and end apart: 2, of which 2 were waited for; matrix products, arithmetic and copies ran while one was open for 0% of the time, Pallas kernels for 0%

commit v1 on v0

--- a/solution.py
+++ b/solution.py
@@ -4,6 +4,28 @@
 from jax.sharding import PartitionSpec as P
 
 TILE = 128
+
+
+def in_order(pieces, dim):
+    lengths = list(pieces.shape[1:])
+    lengths[dim] *= pieces.shape[0]
+    return jnp.moveaxis(pieces, 0, dim).reshape(lengths)
+
+
+def collect(shard, axis, dim):
+    length = lax.axis_size(axis)
+    pairs = [(i, (i + 1) % length) for i in range(length)]
+    back = [(b, a) for a, b in pairs]
+    lower, upper = ([], [])
+    for step in range(length - 1):
+        if step % 2 == 0:
+            lower.append(lax.ppermute(lower[-1] if lower else shard, axis, pairs))
+        else:
+            upper.append(lax.ppermute(upper[-1] if upper else shard, axis, back))
+    blocks = jnp.stack([*lower[::-1], shard, *upper])
+    shift = lax.axis_index(axis) - len(lower)
+    blocks = blocks[(jnp.arange(length) - shift) % length]
+    return in_order(blocks, dim)
 
 
 def expand(values, mask):
@@ -20,9 +42,7 @@
     cols_here = masked_right.shape[1]
     whole_left = lax.all_gather(masked_left, "col", axis=1, tiled=True)
     product = jnp.dot(
-        whole_left,
-        lax.all_gather(masked_right, "row", axis=0, tiled=True),
-        preferred_element_type=jnp.float32,
+        whole_left, collect(masked_right, "row", 0), preferred_element_type=jnp.float32
     )
     kept = expand(product, result_mask).astype(jnp.bfloat16)
     n_row = lax.axis_size("row")

time: 326 us -> 296 us (0.908)
  waiting for transfers between devices: 209 us -> 88.7 us
  local copies, waits for them, and re-layouts: 23.4 us -> 77.4 us
  other arithmetic: 18.4 us -> 32.5 us
  starting transfers between devices: 0.04 us -> 14 us
  blocking collectives: 38.3 us -> 42.3 us
  matrix products: 22.4 us -> 26.3 us
    all_gather x1, waiting for transfers between devices: 122 us -> 0.01 us  [local(): whole_left = lax.all_gather(masked_left, 'col', axis=1, tiled=True)]
    ppermute x0 -> x7, waiting for transfers between devices: none -> 88.7 us  [the longest x4 87.5 us: collect(): lower.append(lax.ppermute(lower[-1] if lower else shard, axis, pairs))]
    all_gather x1 -> x0, waiting for transfers between devices: 87.2 us -> none  [local(): lax.all_gather(masked_right, 'row', axis=0, tiled=True)]
    gather x0 -> x3, local copies, waits for them, and re-layouts: none -> 22.5 us  [collect(): blocks = blocks[(jnp.arange(length) - shift) % length]]
    reshape x0 -> x1, local copies, waits for them, and re-layouts: none -> 21.3 us  [in_order(): return jnp.moveaxis(pieces, 0, dim).reshape(lengths)]
    ppermute x0 -> x7, starting transfers between devices: none -> 14 us  [the longest x4 10.6 us: collect(): lower.append(lax.ppermute(lower[-1] if lower else shard, axis, pairs))]
    unnamed x0 -> x1, other arithmetic: none -> 13.7 us
    all_to_all x1 -> x0, other arithmetic: 13.2 us -> none  [local(): lax.all_to_all(pieces, ('row', 'col'), split_axis=0, concat_axis=0, tiled...]
  transfers between devices with their start and end apart: 2 -> 8, of which waited for: 2 -> 6; matrix products, arithmetic and copies ran while one was open for 0% -> 23% of each run, Pallas kernels for 0% -> 0%
where the time goes in v1:
time: 296 us; the launch traced here: 295 us
  waiting for transfers between devices  88.7 us (30%)
  local copies, waits for them, and re-layouts  77.4 us (26%)
  blocking collectives  42.3 us (14%)
  other arithmetic  32.5 us (11%)
  matrix products  26.3 us (9%)
  starting transfers between devices  14 us (5%)
  between operations  13.5 us (5%)
    ppermute x4, waiting for transfers between devices, collect(): lower.append(lax.ppermute(lower[-1] if lower else shard, axis, pairs))  87.5 us
    all_to_all x1, blocking collectives, local(): lax.all_to_all(pieces, ('row', 'col'), split_axis=0, concat_axis=0, tiled...  42.3 us
    dot_general x1, matrix products, local(): jnp.dot(whole_left, collect(masked_right, 'row', 0), preferred_element_ty...  26.3 us
    unnamed x20, local copies, waits for them, and re-layouts  23.1 us
    gather x3, local copies, waits for them, and re-layouts, collect(): blocks = blocks[(jnp.arange(length) - shift) % length]  22.5 us
    reshape x1, local copies, waits for them, and re-layouts, in_order(): return jnp.moveaxis(pieces, 0, dim).reshape(lengths)  21.3 us
    unnamed x1, other arithmetic  13.7 us
    convert_element_type x1, other arithmetic, local(): kept = expand(product, result_mask).astype(jnp.bfloat16)  13.2 us
  transfers between devices with their start and end apart: 8, of which 6 were waited for; matrix products, arithmetic and copies ran while one was open for 23% of the time, Pallas kernels for 0%

profile of v1, /device:TPU:1, one launch (start us, length us, event | category | flops | bytes accessed | tf_op | source)
XLA Modules:
  0.0 294.9 jit_solution(7676039028394510990)
XLA Ops:
  6.5 0.0 all-gather.2.cloned.1.call-start
  6.5 0.7 convert_element_type.23
  7.2 0.1 copy.15
  7.3 0.3 mul.34
  7.7 2.4 bitcast_multiply_fusion.1
  10.0 0.0 all-gather.2.cloned.1.call-update
  10.1 0.7 convert_element_type.24
  10.8 0.3 mul.37
  11.1 1.9 bitcast_multiply_fusion
  13.0 3.0 %collective-permute-start = (bf16[1024,1024]{1,0:T(8,128)(2,1)S(1)}, bf16[1024,1024]{1,0:T(8,128)(2,1)S(1)}, u32[]{:S(2)}, u32[]{:S(2)}) collective-permute-start(bf16[1024,1024]{1,0:T(8,128)(2,1)S(1)} %bitcast_multiply_fusion), channel_id=1, source_target_pairs={{0,16},{16,32},{32,48},{48,64},{64,80},{80,96},{96,112},{112,0},{1... | collective-permute-start | bytes 6291464 | tf_op jit(solution)/shard_map/ppermute | solution.py:22
  16.0 23.0 %collective-permute-done = bf16[1024,1024]{1,0:T(8,128)(2,1)S(1)} collective-permute-done((bf16[1024,1024]{1,0:T(8,128)(2,1)S(1)}, bf16[1024,1024]{1,0:T(8,128)(2,1)S(1)}, u32[]{:S(2)}, u32[]{:S(2)}) %collective-permute-start) | collective-permute-done | bytes 2097184 | tf_op jit(solution)/shard_map/ppermute | solution.py:22
  39.0 2.5 collective-permute-start.1
  41.5 0.2 collective-permute-start.4
  41.7 22.8 %collective-permute-done.1 = bf16[1024,1024]{1,0:T(8,128)(2,1)S(1)} collective-permute-done((bf16[1024,1024]{1,0:T(8,128)(2,1)S(1)}, bf16[1024,1024]{1,0:T(8,128)(2,1)S(1)}, u32[]{:S(2)}, u32[]{:S(2)}) %collective-permute-start.1) | collective-permute-done | bytes 2097184 | tf_op jit(solution)/shard_map/ppermute | solution.py:22
  64.5 2.5 collective-permute-start.2
  66.9 0.4 collective-permute-done.4
  67.3 0.0 copy-done
  67.3 1.1 collective-permute-start.5
  68.4 0.0 copy-done.2
  68.4 21.5 %collective-permute-done.2 = bf16[1024,1024]{1,0:T(8,128)(2,1)} collective-permute-done((bf16[1024,1024]{1,0:T(8,128)(2,1)S(1)}, bf16[1024,1024]{1,0:T(8,128)(2,1)}, u32[]{:S(2)}, u32[]{:S(2)}) %collective-permute-start.2) | collective-permute-done | bytes 2097184 | tf_op jit(solution)/shard_map/ppermute | solution.py:22
  89.9 2.6 collective-permute-start.3
  92.6 0.9 collective-permute-done.5
  93.4 2.2 collective-permute-start.6
  95.6 20.2 %collective-permute-done.3 = bf16[1024,1024]{1,0:T(8,128)(2,1)} collective-permute-done((bf16[1024,1024]{1,0:T(8,128)(2,1)}, bf16[1024,1024]{1,0:T(8,128)(2,1)}, u32[]{:S(2)}, u32[]{:S(2)}) %collective-permute-start.3) | collective-permute-done | bytes 2097184 | tf_op jit(solution)/shard_map/ppermute | solution.py:22
  115.8 1.9 bitcast_dynamic-update-slice_fusion.7
  117.7 1.9 bitcast_dynamic-update-slice_fusion.6
  119.5 0.2 bitcast_dynamic-update-slice_fusion.5
  119.7 0.0 copy-done.1
  119.7 0.2 bitcast_dynamic-update-slice_fusion.4
  119.9 0.2 bitcast_dynamic-update-slice_fusion.3
  120.1 1.8 bitcast_dynamic-update-slice_fusion.2
  121.9 1.8 bitcast_dynamic-update-slice_fusion.1
  123.7 0.0 collective-permute-done.6
  123.7 0.2 bitcast_dynamic-update-slice_fusion
  123.8 6.4 %fusion.2 = (bf16[8,512,1024]{2,1,0:T(8,128)(2,1)}, bf16[8,512,1024]{2,1,0:T(8,128)(2,1)}) fusion(bf16[8,1024,1024]{2,1,0:T(8,128)(2,1)S(1)} %bitcast_dynamic-update-slice_fusion), kind=kLoop, calls=%fused_computation.22 | loop fusion | bytes 33554432 | tf_op jit(solution)/shard_map/gather | solution.py:27
  130.2 8.0 %gather_fusion = bf16[8,512,1024]{2,1,0:T(8,128)(2,1)} fusion(bf16[8,512,1024]{2,1,0:T(8,128)(2,1)} %get-tuple-element.5, s32[1024]{0:T(1024)S(1)} %pad_clamp_fusion), kind=kCustom, calls=%fused_computation | custom fusion | bytes 16777248 | tf_op jit(solution)/shard_map/gather | solution.py:27
  138.3 8.0 %gather_fusion.1 = bf16[8,512,1024]{2,1,0:T(8,128)(2,1)} fusion(bf16[8,512,1024]{2,1,0:T(8,128)(2,1)} %get-tuple-element.6, s32[1024]{0:T(1024)S(1)} %pad_clamp_fusion), kind=kCustom, calls=%fused_computation.1 | custom fusion | bytes 16777248 | tf_op jit(solution)/shard_map/gather | solution.py:27
  146.3 13.7 %pad_maximum_fusion = bf16[8,1024,1024]{2,1,0:T(8,128)(2,1)} fusion(bf16[8,512,1024]{2,1,0:T(8,128)(2,1)} %gather_fusion.1, bf16[8,512,1024]{2,1,0:T(8,128)(2,1)} %gather_fusion), kind=kLoop, calls=%fused_computation.2 | loop fusion | flops 33554432 | bytes 33554432
  160.0 21.3 %copy.16 = bf16[8192,1024]{0,1:T(8,128)(2,1)} copy(bf16[8192,1024]{1,0:T(8,128)(2,1)} %bitcast.44) | data formatting | bytes 33554432 | tf_op jit(solution)/shard_map/reshape | solution.py:12
  181.3 26.3 %multiply_convert_fusion = bf16[8,128,8,128]{3,1,2,0:T(8,128)(2,1)} fusion(bf16[8,128,8192,1]{2,1,3,0:T(8,128)(2,1)} %bitcast.48, bf16[8,128,8192,1]{2,1,0,3:T(8,128)(2,1)} %bitcast.45, f32[8,8]{1,0:T(8,128)S(1)} %convert_element_type.25), kind=kOutput, calls=%fused_computation.3 | convolution fusion | flops 17181966336 | bytes 35651840 | tf_op jit(solution)/shard_map/dot_general | solution.py:44
  207.6 3.0 %copy.17 = bf16[8,128,8,128]{3,2,1,0:T(8,128)(2,1)S(1)} copy(bf16[8,128,8,128]{3,1,2,0:T(8,128)(2,1)} %multiply_convert_fusion) | data formatting | bytes 4194304 | tf_op jit(solution)/shard_map/convert_element_type | solution.py:47
  210.5 6.2 %convert_element_type.28 = bf16[128,1,8192]{2,1,0:T(2,128)(2,1)} reshape(bf16[8,128,8,128]{3,2,1,0:T(8,128)(2,1)S(1)} %copy.17) | data formatting | bytes 4194304 | tf_op jit(solution)/shard_map/convert_element_type | solution.py:47
  216.7 0.5 broadcast.78
  217.2 13.2 %reduce = bf16[128,8192]{1,0:T(8,128)(2,1)S(1)} reduce(bf16[128,1,8192]{2,1,0:T(2,128)(2,1)} %convert_element_type.28, bf16[]{:T(256)} %broadcast.78), dimensions={1}, to_apply=%convert_element_type.28.reduce_sub_computation | reduce | bytes 4194306 | tf_op jit(solution)/shard_map/convert_element_type | solution.py:47
  230.5 2.8 reshape.105
  233.2 42.3 %all_to_all.9 = bf16[128,2,4096]{2,1,0:T(2,128)(2,1)S(1)} all-to-all(bf16[128,2,4096]{2,1,0:T(2,128)(2,1)} %reshape.105), channel_id=1, replica_groups=mesh['row'=8,'col'=16] {'row','col'}, dimensions={0} | all-to-all | bytes 4194304 | tf_op jit(solution)/shard_map/all_to_all | solution.py:53
  275.6 6.7 %reshape.106 = bf16[128,1,8192]{2,1,0:T(2,128)(2,1)} reshape(bf16[128,2,4096]{2,1,0:T(2,128)(2,1)S(1)} %all_to_all.9) | data formatting | bytes 4194304
  282.3 5.8 %copy.26 = bf16[128,1,8192]{2,0,1:T(8,128)(2,1)} copy(bf16[128,1,8192]{2,1,0:T(2,128)(2,1)} %reshape.106) | data formatting | bytes 4194304
  (11 shorter events, 0.0 us)
Async XLA Ops:
  6.5 86.0 %copy-start.4 = (s32[8,8]{1,0:T(8,128)S(1)}, s32[8,8]{1,0:T(8,128)}, u32[]{:S(2)}) copy-start(s32[8,8]{1,0:T(8,128)} %param.9) | copy-start | bytes 772
  6.5 174.7 %all-gather.2.cloned.1.call-start = ((), (), s32[]{:S(2)}) async-start(), calls=%async_computation.1 | async-start | bytes 17825792 | tf_op jit(solution)/shard_map/all_gather | solution.py:43
  13.0 26.0 %collective-permute-start = (bf16[1024,1024]{1,0:T(8,128)(2,1)S(1)}, bf16[1024,1024]{1,0:T(8,128)(2,1)S(1)}, u32[]{:S(2)}, u32[]{:S(2)}) collective-permute-start(bf16[1024,1024]{1,0:T(8,128)(2,1)S(1)} %bitcast_multiply_fusion), channel_id=1, source_target_pairs={{0,16},{16,32},{32,48},{48,64},{64,80},{80,96},{96,112},{112,0},{1... | collective-permute-start | bytes 6291464 | tf_op jit(solution)/shard_map/ppermute | solution.py:22
  39.0 28.3 %copy-start = (bf16[1024,1024]{1,0:T(8,128)(2,1)}, bf16[1024,1024]{1,0:T(8,128)(2,1)S(1)}, u32[]{:S(2)}) copy-start(bf16[1024,1024]{1,0:T(8,128)(2,1)S(1)} %collective-permute-done) | copy-start | bytes 6291460
  39.0 25.5 %collective-permute-start.1 = (bf16[1024,1024]{1,0:T(8,128)(2,1)S(1)}, bf16[1024,1024]{1,0:T(8,128)(2,1)S(1)}, u32[]{:S(2)}, u32[]{:S(2)}) collective-permute-start(bf16[1024,1024]{1,0:T(8,128)(2,1)S(1)} %collective-permute-done), channel_id=1, source_target_pairs={{0,16},{16,32},{32,48},{48,64},{64,80},{80,96},{96,112},{112,0},{1... | collective-permute-start | bytes 6291464 | tf_op jit(solution)/shard_map/ppermute | solution.py:22
  41.5 25.9 %collective-permute-start.4 = (bf16[1024,1024]{1,0:T(8,128)(2,1)S(1)}, bf16[1024,1024]{1,0:T(8,128)(2,1)}, u32[]{:S(2)}, u32[]{:S(2)}) collective-permute-start(bf16[1024,1024]{1,0:T(8,128)(2,1)S(1)} %bitcast_multiply_fusion), channel_id=1, source_target_pairs={{16,0},{32,16},{48,32},{64,48},{80,64},{96,80},{112,96},{0,112},{1... | collective-permute-start | bytes 6291464 | tf_op jit(solution)/shard_map/ppermute | solution.py:24
  64.5 3.9 %copy-start.2 = (bf16[1024,1024]{1,0:T(8,128)(2,1)}, bf16[1024,1024]{1,0:T(8,128)(2,1)S(1)}, u32[]{:S(2)}) copy-start(bf16[1024,1024]{1,0:T(8,128)(2,1)S(1)} %collective-permute-done.1) | copy-start | bytes 6291460
  64.5 25.5 %collective-permute-start.2 = (bf16[1024,1024]{1,0:T(8,128)(2,1)S(1)}, bf16[1024,1024]{1,0:T(8,128)(2,1)}, u32[]{:S(2)}, u32[]{:S(2)}) collective-permute-start(bf16[1024,1024]{1,0:T(8,128)(2,1)S(1)} %collective-permute-done.1), channel_id=1, source_target_pairs={{0,16},{16,32},{32,48},{48,64},{64,80},{80,96},{96,112},{112,0},{1... | collective-permute-start | bytes 6291464 | tf_op jit(solution)/shard_map/ppermute | solution.py:22
  67.3 26.1 %collective-permute-start.5 = (bf16[1024,1024]{1,0:T(8,128)(2,1)}, bf16[1024,1024]{1,0:T(8,128)(2,1)}, u32[]{:S(2)}, u32[]{:S(2)}) collective-permute-start(bf16[1024,1024]{1,0:T(8,128)(2,1)} %collective-permute-done.4), channel_id=1, source_target_pairs={{16,0},{32,16},{48,32},{64,48},{80,64},{96,80},{112,96},{0,112},{1... | collective-permute-start | bytes 6291464 | tf_op jit(solution)/shard_map/ppermute | solution.py:24
  89.9 25.9 %collective-permute-start.3 = (bf16[1024,1024]{1,0:T(8,128)(2,1)}, bf16[1024,1024]{1,0:T(8,128)(2,1)}, u32[]{:S(2)}, u32[]{:S(2)}) collective-permute-start(bf16[1024,1024]{1,0:T(8,128)(2,1)} %collective-permute-done.2), channel_id=1, source_target_pairs={{0,16},{16,32},{32,48},{48,64},{64,80},{80,96},{96,112},{112,0},{1... | collective-permute-start | bytes 6291464 | tf_op jit(solution)/shard_map/ppermute | solution.py:22
  92.5 27.0 %copy-start.3 = (bf16[1024,1024]{1,0:T(8,128)(2,1)S(1)}, bf16[1024,1024]{1,0:T(8,128)(2,1)}, u32[]{:S(2)}) copy-start(bf16[1024,1024]{1,0:T(8,128)(2,1)} %copy-done.2) | copy-start | bytes 6291460
  92.5 27.2 %copy-start.1 = (bf16[1024,1024]{1,0:T(8,128)(2,1)S(1)}, bf16[1024,1024]{1,0:T(8,128)(2,1)}, u32[]{:S(2)}) copy-start(bf16[1024,1024]{1,0:T(8,128)(2,1)} %copy-done) | copy-start | bytes 6291460
  93.4 30.2 %collective-permute-start.6 = (bf16[1024,1024]{1,0:T(8,128)(2,1)}, bf16[1024,1024]{1,0:T(8,128)(2,1)S(1)}, u32[]{:S(2)}, u32[]{:S(2)}) collective-permute-start(bf16[1024,1024]{1,0:T(8,128)(2,1)} %collective-permute-done.5), channel_id=1, source_target_pairs={{16,0},{32,16},{48,32},{64,48},{80,64},{96,80},{112,96},{0,112},{1... | collective-permute-start | bytes 6291464 | tf_op jit(solution)/shard_map/ppermute | solution.py:24
Sparse Core Ops, SparseCore 0:
  10.2 123.2 all-gather.1
